TPU v7x, 32 devices: a whole 2x2x4 slice. The times are simulated.
32 devices in a mesh: groups: 2 (over x), region: 16 (over z, y, core).
Axes of the slice: x: 2, y: 2, z: 4, core: 2. Of those that a mesh axis runs over, the one named last changes fastest.
Arguments:
- record: bfloat16 [16384, 640], P(('groups', 'region')), parts along dimension 0, may hold values from -6 to 6
- target: bfloat16 [4, 16384, 8192], P(None, ('groups', 'region')), parts along dimension 1, may hold values from -0.59765625 to 0.59765625
- offset: int32 [2], P('groups'), parts along dimension 0, may hold values from 0 to 127
- lag_steps: int32 [6], P('groups'), parts along dimension 0, may hold values from 1 to 8
Outputs:
- grad: float32 [16384, 640], P(('groups', 'region')), parts along dimension 0
There are 2 independent parts, one for each index of `groups`. A program takes and returns all parts, laid end to end along the dimension named above; each array names one. Nothing has to cross between parts.
All inputs are finite; a program needn't handle non-finite values.
Results may differ from a plain program's by a relative error of at most 0.0005.
Values may be sent and summed in bfloat16 or wider, within the bound.
A program may use at most 256 MiB of HBM per device.

v0:
```python
import jax
import jax.numpy as jnp
from jax import lax
from jax.sharding import PartitionSpec as P

REGIONS = 8192
SAMPLES = 384
SLACK = 128
LAGS = 3


def shifted(value, axis, steps):
    count = lax.axis_size(axis)
    pairs = [(source, (source + steps) % count) for source in range(count)]
    return lax.ppermute(value, axis, pairs)


def outer_dot(left, right):
    return lax.dot_general(
        left, right, (((1,), (1,)), ((), ())), preferred_element_type=jnp.float32
    )


def split_views(window, lag_steps):
    early_view = window[:, :SAMPLES]
    later_list = []
    for lag_number in range(LAGS):
        later_list.append(lax.dynamic_slice_in_dim(window, lag_steps[lag_number], SAMPLES, 1))
    return (early_view, jnp.stack(later_list))


def place_views(early_part, later_parts, lag_steps, win_width):
    block_rows = early_part.shape[0]
    placed = jnp.pad(early_part, ((0, 0), (0, win_width - SAMPLES)))
    blank = jnp.zeros((block_rows, win_width), jnp.float32)
    for lag_number in range(LAGS):
        placed = placed + lax.dynamic_update_slice(
            blank, later_parts[lag_number], (0, lag_steps[lag_number])
        )
    return placed


def pair_tiles(own_views, other_views, target, flipped, column_at, width, factor):
    inverse = 1.0 / SAMPLES
    weight = SAMPLES / REGIONS
    own_early, own_later = own_views
    other_early, other_later = other_views
    tiles = lax.dynamic_slice_in_dim(target, column_at, width, 2).astype(jnp.float32)
    mirror = lax.dynamic_slice_in_dim(flipped, column_at, width, 2).astype(jnp.float32)
    cov_zero = outer_dot(own_early, other_early) * inverse
    cov_fore = (
        jnp.einsum("rs,lcs->lrc", own_early, other_later, preferred_element_type=jnp.float32)
        * inverse
    )
    cov_back = (
        jnp.einsum("lrs,cs->lrc", own_later, other_early, preferred_element_type=jnp.float32)
        * inverse
    )
    sym_err = (weight * (2.0 * cov_zero - tiles[0] - mirror[0]) * factor).astype(jnp.bfloat16)
    fore_err = (weight * (cov_fore - tiles[1:]) * factor).astype(jnp.bfloat16)
    back_err = (weight * (cov_back - mirror[1:]) * factor).astype(jnp.bfloat16)
    return (sym_err, fore_err, back_err)


def own_terms(errors, other_views):
    sym_err, fore_err, back_err = errors
    other_early, other_later = other_views
    to_early = jnp.dot(sym_err, other_early, preferred_element_type=jnp.float32)
    to_early = to_early + jnp.einsum(
        "lrc,lcs->rs", fore_err, other_later, preferred_element_type=jnp.float32
    )
    to_later = jnp.einsum("lrc,cs->lrs", back_err, other_early, preferred_element_type=jnp.float32)
    return (to_early, to_later)


def other_terms(errors, own_views):
    sym_err, fore_err, back_err = errors
    own_early, own_later = own_views
    to_early = jnp.einsum("rc,rs->cs", sym_err, own_early, preferred_element_type=jnp.float32)
    to_early = to_early + jnp.einsum(
        "lrc,lrs->cs", back_err, own_later, preferred_element_type=jnp.float32
    )
    to_later = jnp.einsum("lrc,rs->lcs", fore_err, own_early, preferred_element_type=jnp.float32)
    return (to_early, to_later)


def shards(record, target, offset, lag_steps):
    block_rows = record.shape[0]
    begin_at = offset[0]
    win_width = SAMPLES + SLACK
    window = lax.dynamic_slice_in_dim(record, begin_at, win_width, 1)
    own_views = split_views(window, lag_steps)
    devices = lax.axis_size("region")
    own_index = lax.axis_index("region")
    stacked = target.shape[0]
    received = lax.all_to_all(target, "region", split_axis=2, concat_axis=2, tiled=True)
    flipped = (
        received.reshape(stacked, block_rows, devices, block_rows)
        .transpose(0, 3, 2, 1)
        .reshape(stacked, block_rows, devices * block_rows)
    )
    errors = pair_tiles(
        own_views, own_views, target, flipped, own_index * block_rows, block_rows, 1.0
    )
    grad_early, grad_later = own_terms(errors, own_views)
    halfway = devices // 2

    def visit_block(step_number, loop_state):
        visitor, partials, grad_early, grad_later = loop_state
        visitor = shifted(visitor, "region", 1)
        partials = shifted(partials, "region", 1)
        block_id = (own_index - step_number + devices) % devices
        factor = jnp.where(step_number == halfway, 0.5, 1.0)
        other_views = split_views(visitor, lag_steps)
        errors = pair_tiles(
            own_views, other_views, target, flipped, block_id * block_rows, block_rows, factor
        )
        add_early, add_later = own_terms(errors, other_views)
        to_early, to_later = other_terms(errors, own_views)
        partials = partials + place_views(to_early, to_later, lag_steps, win_width)
        return (visitor, partials, grad_early + add_early, grad_later + add_later)

    def visit_four(turn_number, loop_state):
        for inner in range(4):
            loop_state = visit_block(1 + 4 * turn_number + inner, loop_state)
        return loop_state

    start_state = (window, jnp.zeros((block_rows, win_width), jnp.float32), grad_early, grad_later)
    final_state = lax.fori_loop(0, halfway // 4, visit_four, start_state)
    returned = shifted(final_state[1], "region", halfway)
    in_window = place_views(final_state[2], final_state[3], lag_steps, win_width) + returned
    grad = lax.dynamic_update_slice(jnp.zeros(record.shape, jnp.float32), in_window, (0, begin_at))
    return grad


def solution(mesh):
    placed = (
        P(("groups", "region"), None),
        P(None, ("groups", "region"), None),
        P("groups"),
        P("groups"),
    )
    return jax.shard_map(
        shards, mesh=mesh, in_specs=placed, out_specs=P(("groups", "region"), None), check_vma=False
    )
```

profile of v0, /device:TPU:0, one launch (start us, length us, event | category | flops | bytes accessed | tf_op | source)
XLA Modules:
  0.0 1366.3 jit_solution(1209809443540427602)
XLA Ops:
  0.0 54.7 %copy.41 = bf16[4,512,8192]{1,0,2:T(4,128)(2,1)} copy(bf16[4,512,8192]{2,1,0:T(8,128)(2,1)} %param.7) | data formatting | bytes 67108864 | tf_op args[1]
  54.7 7.6 all-to-all-start
  82.9 568.3 %all-to-all-done = bf16[4,512,8192]{1,0,2:T(4,128)(2,1)} async-done(((bf16[4,512,8192]{1,0,2:T(4,128)(2,1)}), bf16[4,512,8192]{1,0,2:T(4,128)(2,1)}, u32[]{:S(2)}, u32[]{:S(2)}) %all-to-all-start) | async-done | bytes 33554464 | tf_op jit(solution)/shard_map/all_to_all | solution.py:96
  651.2 31.1 %copy.58 = bf16[4,512,16,512]{1,2,3,0:T(8,128)(2,1)} copy(bf16[4,512,16,512]{1,0,3,2:T(4,128)(2,1)} %bitcast.2) | data formatting | bytes 67108864 | tf_op jit(solution)/shard_map/reshape | solution.py:98
  682.3 50.0 %reshape.7 = bf16[4,512,8192]{2,1,0:T(8,128)(2,1)} reshape(bf16[4,512,16,512]{3,2,1,0:T(8,128)(2,1)} %bitcast.439) | data formatting | bytes 67108864 | tf_op jit(solution)/shard_map/reshape | solution.py:100
  742.2 569.7 %while.23 = (s32[]{:T(128)}, bf16[512,512]{1,0:T(8,128)(2,1)S(1)}, f32[512,512]{1,0:T(8,128)}, f32[512,384]{1,0:T(8,128)}, f32[3,512,384]{2,1,0:T(8,128)}, /*ind...) while((s32[]{:T(128)}, bf16[512,512]{1,0:T(8,128)(2,1)S(1)}, ...), condition=%wide.region_1.2_spmd.clone, body=%wide.region_0.1_spmd.clone.sunk | while | flops 16968056832 | bytes 541067456 | solution.py:129
  744.3 44.9 %collective-permute-start.4 = (f32[512,512]{1,0:T(8,128)}, f32[512,512]{1,0:T(8,128)}, u32[]{:S(2)}, u32[]{:S(2)}) collective-permute-start(f32[512,512]{1,0:T(8,128)} %broadcast_select_fusion.2), channel_id=1, source_target_pairs={{0,1},{1,2},{2,3},{3,4},{4,5},{5,6},{6,7},{7,8},{8,9},{9,10},{10,1... | collective-permute-start | bytes 3145736 | tf_op jit(solution)/shard_map/while/body/eval_jaxpr/ppermute | solution.py:15
  789.2 15.5 %dynamic-slice_convert_fusion.11 = (f32[4,512,512]{2,1,0:T(8,128)}, f32[4,512,512]{2,1,0:T(8,128)}, f32[4,512,512]{2,1,0:T(8,128)}, f32[4,512,512]{2,1,0:T(8,128...) fusion(bf16[4,512,8192]{2,1,0:T(8,128)(2,1)} %get-tuple-element, ...), kind=kLoop, calls=%fused_computation.25.clone.1 | loop fusion | flops 8388608 | bytes 50331664 | tf_op jit(solution)/shard_map/while/body/eval_jaxpr/convert_element_type | solution.py:49
  804.7 80.8 %collective-permute-done = bf16[512,512]{1,0:T(8,128)(2,1)S(1)} collective-permute-done((bf16[512,512]{1,0:T(8,128)(2,1)S(1)}, bf16[512,512]{1,0:T(8,128)(2,1)S(1)}, u32[]{:S(2)}, u32[]{:S(2)}) %collective-permute-start) | collective-permute-done | bytes 524320 | tf_op jit(solution)/shard_map/while/body/eval_jaxpr/ppermute | solution.py:15
  896.0 3.6 copy.60
  899.6 3.7 fusion.327
  910.2 5.2 add.905
  918.0 5.2 add.906
  925.9 5.2 add.907
  936.7 11.3 collective-permute-done.1
  961.3 5.2 add.909
  969.2 5.2 add.910
  977.0 5.2 add.911
  988.1 5.9 collective-permute-done.2
  1006.4 5.2 add.913
  1014.2 5.2 add.914
  1022.1 5.2 add.915
  1048.9 6.5 add.917
  1057.7 6.5 add.918
  1072.5 6.5 add.919
  1082.0 6.1 add_add_fusion.2
  1093.6 15.5 %dynamic-slice_convert_fusion.11 = (f32[4,512,512]{2,1,0:T(8,128)}, f32[4,512,512]{2,1,0:T(8,128)}, f32[4,512,512]{2,1,0:T(8,128)}, f32[4,512,512]{2,1,0:T(8,128...) fusion(bf16[4,512,8192]{2,1,0:T(8,128)(2,1)} %get-tuple-element, ...), kind=kLoop, calls=%fused_computation.25.clone.1 | loop fusion | flops 8388608 | bytes 50331664 | tf_op jit(solution)/shard_map/while/body/eval_jaxpr/convert_element_type | solution.py:49
  1123.1 3.7 fusion.327
  1133.8 5.2 add.905
  1141.6 5.2 add.906
  1149.5 5.2 add.907
  1160.4 6.0 collective-permute-done.1
  1179.7 5.2 add.909
  1187.6 5.2 add.910
  1195.4 5.2 add.911
  1206.0 6.1 collective-permute-done.2
  1224.5 5.2 add.913
  1232.4 5.2 add.914
  1240.2 5.2 add.915
  1267.0 6.5 add.917
  1275.8 6.5 add.918
  1290.6 6.5 add.919
  1300.1 6.1 add_add_fusion.2
  1314.8 6.9 add.709
  1323.1 6.9 add.711
  1331.4 6.9 add.713
  1338.3 18.9 %collective-permute-done.8 = f32[512,512]{1,0:T(8,128)} collective-permute-done((f32[512,512]{1,0:T(8,128)}, f32[512,512]{1,0:T(8,128)}, u32[]{:S(2)}, u32[]{:S(2)}) %collective-permute-start.8) | collective-permute-done | bytes 1048608 | tf_op jit(solution)/shard_map/ppermute | solution.py:15
  1359.8 6.1 dynamic_update_slice.75
  (290 shorter events, 255.8 us)
Async XLA Ops:
  54.7 7.6 copy-start.34
  54.7 14.5 %copy-start.32 = (bf16[512,640]{1,0:T(8,128)(2,1)S(1)}, bf16[512,640]{1,0:T(8,128)(2,1)}, u32[]{:S(2)}) copy-start(bf16[512,640]{1,0:T(8,128)(2,1)} %param.6) | copy-start | bytes 1966084
  54.7 596.5 %all-to-all-start = ((bf16[4,512,8192]{1,0,2:T(4,128)(2,1)}), bf16[4,512,8192]{1,0,2:T(4,128)(2,1)}, u32[]{:S(2)}, u32[]{:S(2)}) async-start(bf16[4,512,8192]{1,0,2:T(4,128)(2,1)} %copy.41), calls=%async_computation | async-start | bytes 67108864 | tf_op jit(solution)/shard_map/all_to_all | solution.py:96
  76.6 4.3 copy-start.25
  732.2 4.4 copy-start.27
  742.4 143.1 %collective-permute-start = (bf16[512,512]{1,0:T(8,128)(2,1)S(1)}, bf16[512,512]{1,0:T(8,128)(2,1)S(1)}, u32[]{:S(2)}, u32[]{:S(2)}) collective-permute-start(bf16[512,512]{1,0:T(8,128)(2,1)S(1)} %get-tuple-element.604), channel_id=1, source_target_pairs={{0,1},{1,2},{2,3},{3,4},{4,5},{5,6},{6,7},{7,8},{8,9},{9,10},{10,1... | collective-permute-start | bytes 1572872 | tf_op jit(solution)/shard_map/while/body/eval_jaxpr/ppermute | solution.py:15
  744.3 208.1 %collective-permute-start.4 = (f32[512,512]{1,0:T(8,128)}, f32[512,512]{1,0:T(8,128)}, u32[]{:S(2)}, u32[]{:S(2)}) collective-permute-start(f32[512,512]{1,0:T(8,128)} %broadcast_select_fusion.2), channel_id=1, source_target_pairs={{0,1},{1,2},{2,3},{3,4},{4,5},{5,6},{6,7},{7,8},{8,9},{9,10},{10,1... | collective-permute-start | bytes 3145736 | tf_op jit(solution)/shard_map/while/body/eval_jaxpr/ppermute | solution.py:15
  903.2 3.1 copy-start.16
  931.1 3.1 copy-start.17
  931.1 16.8 %collective-permute-start.1 = (bf16[512,512]{1,0:T(8,128)(2,1)S(1)}, bf16[512,512]{1,0:T(8,128)(2,1)S(1)}, u32[]{:S(2)}, u32[]{:S(2)}) collective-permute-start(bf16[512,512]{1,0:T(8,128)(2,1)S(1)} %collective-permute-done), channel_id=1, source_target_pairs={{0,1},{1,2},{2,3},{3,4},{4,5},{5,6},{6,7},{7,8},{8,9},{9,10},{10,1... | collective-permute-start | bytes 1572872 | tf_op jit(solution)/shard_map/while/body/eval_jaxpr/ppermute | solution.py:15
  934.2 14.2 %copy-start.11 = (f32[4,512,512]{2,1,0:T(8,128)S(1)}, f32[4,512,512]{2,1,0:T(8,128)}, u32[]{:S(2)}) copy-start(f32[4,512,512]{2,1,0:T(8,128)} %get-tuple-element.562) | copy-start | bytes 12582916 | tf_op jit(solution)/shard_map/while
  949.5 2.9 copy-start.4
  951.4 4.5 copy-start.2
  952.4 7.7 copy-start.5
  955.9 77.9 %collective-permute-start.5 = (f32[512,512]{1,0:T(8,128)}, f32[512,512]{1,0:T(8,128)}, u32[]{:S(2)}, u32[]{:S(2)}) collective-permute-start(f32[512,512]{1,0:T(8,128)} %add.908), channel_id=1, source_target_pairs={{0,1},{1,2},{2,3},{3,4},{4,5},{5,6},{6,7},{7,8},{8,9},{9,10},{10,1... | collective-permute-start | bytes 3145736 | tf_op jit(solution)/shard_map/while/body/eval_jaxpr/ppermute | solution.py:15
  982.2 3.5 copy-start.15
  982.2 11.7 collective-permute-start.2
  985.7 8.3 copy-start.1
  995.0 3.3 copy-start.12
  1027.3 11.3 collective-permute-start.3
  1031.4 7.2 copy-start
  1036.5 31.3 %collective-permute-start.6 = (f32[512,512]{1,0:T(8,128)}, f32[512,512]{1,0:T(8,128)}, u32[]{:S(2)}, u32[]{:S(2)}) collective-permute-start(f32[512,512]{1,0:T(8,128)} %add.912), channel_id=1, source_target_pairs={{0,1},{1,2},{2,3},{3,4},{4,5},{5,6},{6,7},{7,8},{8,9},{9,10},{10,1... | collective-permute-start | bytes 3145736 | tf_op jit(solution)/shard_map/while/body/eval_jaxpr/ppermute | solution.py:15
  1039.7 3.3 copy-start.18
  1064.2 3.6 copy-start.3
  1070.2 17.9 %collective-permute-start.7 = (f32[512,512]{1,0:T(8,128)}, f32[512,512]{1,0:T(8,128)}, u32[]{:S(2)}, u32[]{:S(2)}) collective-permute-start(f32[512,512]{1,0:T(8,128)} %add.916), channel_id=1, source_target_pairs={{0,1},{1,2},{2,3},{3,4},{4,5},{5,6},{6,7},{7,8},{8,9},{9,10},{10,1... | collective-permute-start | bytes 3145736 | tf_op jit(solution)/shard_map/while/body/eval_jaxpr/ppermute | solution.py:15
  1079.0 3.0 copy-start.8
  1090.7 18.3 %collective-permute-start = (bf16[512,512]{1,0:T(8,128)(2,1)S(1)}, bf16[512,512]{1,0:T(8,128)(2,1)S(1)}, u32[]{:S(2)}, u32[]{:S(2)}) collective-permute-start(bf16[512,512]{1,0:T(8,128)(2,1)S(1)} %get-tuple-element.604), channel_id=1, source_target_pairs={{0,1},{1,2},{2,3},{3,4},{4,5},{5,6},{6,7},{7,8},{8,9},{9,10},{10,1... | collective-permute-start | bytes 1572872 | tf_op jit(solution)/shard_map/while/body/eval_jaxpr/ppermute | solution.py:15
  1093.5 77.4 %collective-permute-start.4 = (f32[512,512]{1,0:T(8,128)}, f32[512,512]{1,0:T(8,128)}, u32[]{:S(2)}, u32[]{:S(2)}) collective-permute-start(f32[512,512]{1,0:T(8,128)} %broadcast_select_fusion.2), channel_id=1, source_target_pairs={{0,1},{1,2},{2,3},{3,4},{4,5},{5,6},{6,7},{7,8},{8,9},{9,10},{10,1... | collective-permute-start | bytes 3145736 | tf_op jit(solution)/shard_map/while/body/eval_jaxpr/ppermute | solution.py:15
  1126.8 3.1 copy-start.16
  1154.7 3.3 copy-start.17
  1154.7 11.7 collective-permute-start.1
  1158.0 8.9 copy-start.11
  1168.0 2.9 copy-start.4
  1169.9 4.5 copy-start.2
  1170.9 7.7 copy-start.5
  1174.4 77.6 %collective-permute-start.5 = (f32[512,512]{1,0:T(8,128)}, f32[512,512]{1,0:T(8,128)}, u32[]{:S(2)}, u32[]{:S(2)}) collective-permute-start(f32[512,512]{1,0:T(8,128)} %add.908), channel_id=1, source_target_pairs={{0,1},{1,2},{2,3},{3,4},{4,5},{5,6},{6,7},{7,8},{8,9},{9,10},{10,1... | collective-permute-start | bytes 3145736 | tf_op jit(solution)/shard_map/while/body/eval_jaxpr/ppermute | solution.py:15
  1200.6 3.0 copy-start.15
  1200.6 11.5 collective-permute-start.2
  1203.7 8.4 copy-start.1
  1213.2 3.3 copy-start.12
  1245.5 11.3 collective-permute-start.3
  1249.5 7.2 copy-start
  1254.7 31.3 %collective-permute-start.6 = (f32[512,512]{1,0:T(8,128)}, f32[512,512]{1,0:T(8,128)}, u32[]{:S(2)}, u32[]{:S(2)}) collective-permute-start(f32[512,512]{1,0:T(8,128)} %add.912), channel_id=1, source_target_pairs={{0,1},{1,2},{2,3},{3,4},{4,5},{5,6},{6,7},{7,8},{8,9},{9,10},{10,1... | collective-permute-start | bytes 3145736 | tf_op jit(solution)/shard_map/while/body/eval_jaxpr/ppermute | solution.py:15
  1257.8 3.3 copy-start.18
  1282.4 3.6 copy-start.3
  1288.3 17.9 %collective-permute-start.7 = (f32[512,512]{1,0:T(8,128)}, f32[512,512]{1,0:T(8,128)}, u32[]{:S(2)}, u32[]{:S(2)}) collective-permute-start(f32[512,512]{1,0:T(8,128)} %add.916), channel_id=1, source_target_pairs={{0,1},{1,2},{2,3},{3,4},{4,5},{5,6},{6,7},{7,8},{8,9},{9,10},{10,1... | collective-permute-start | bytes 3145736 | tf_op jit(solution)/shard_map/while/body/eval_jaxpr/ppermute | solution.py:15
  1297.1 3.0 copy-start.8
  1312.0 45.2 %collective-permute-start.8 = (f32[512,512]{1,0:T(8,128)}, f32[512,512]{1,0:T(8,128)}, u32[]{:S(2)}, u32[]{:S(2)}) collective-permute-start(f32[512,512]{1,0:T(8,128)} %get-tuple-element.357), channel_id=1, source_target_pairs={{0,8},{1,9},{2,10},{3,11},{4,12},{5,13},{6,14},{7,15},{8,0},{9,1},... | collective-permute-start | bytes 3145736 | tf_op jit(solution)/shard_map/ppermute | solution.py:15
  (32 other events, 51.4 us)
where the time goes:
time: 1380 us; the launch traced here: 1370 us
  waiting for transfers between devices  701 us (51%)
  local copies, waits for them, and re-layouts  341 us (25%)
  matrix products  130 us (9%)
  other arithmetic  127 us (9%)
  starting transfers between devices  55.9 us (4%)
    all_to_all x1, waiting for transfers between devices, shards(): lax.all_to_all(target, 'region', split_axis=2, concat_axis=2, tiled=True)  568 us
    add x27, local copies, waits for them, and re-layouts, place_views(): placed + lax.dynamic_update_slice(blank, later_parts[lag_number], (0, lag...  153 us
    ppermute x17, waiting for transfers between devices, shifted(): return lax.ppermute(value, axis, pairs)  133 us
    unnamed x17, local copies, waits for them, and re-layouts  58.8 us
    dynamic_update_slice x27, other arithmetic, place_views(): lax.dynamic_update_slice(blank, later_parts[lag_number], (0, lag_steps[la...  56.8 us
    reshape x1, local copies, waits for them, and re-layouts, shards(): flipped = received.reshape(stacked, block_rows, devices, block_rows).tran...  50 us
    ppermute x17, starting transfers between devices, shifted(): return lax.ppermute(value, axis, pairs)  48.3 us
    convert_element_type x3, other arithmetic, pair_tiles(): lax.dynamic_slice_in_dim(flipped, column_at, width, 2).astype(jnp.float32)  33.3 us
  transfers between devices with their start and end apart: 18, of which 9 were waited for; matrix products, arithmetic and copies ran while one was open for 30% of the time, Pallas kernels for 0%

commit v1 on v0

--- a/solution.py
+++ b/solution.py
@@ -93,7 +93,19 @@
     devices = lax.axis_size("region")
     own_index = lax.axis_index("region")
     stacked = target.shape[0]
-    received = lax.all_to_all(target, "region", split_axis=2, concat_axis=2, tiled=True)
+    ways, here = (lax.axis_size("region"), lax.axis_index("region"))
+    width_2 = target.shape[2] // ways
+    dims = list(target.shape)
+    dims[2] = width_2
+    height = dims[2]
+    dims[2] = height * ways
+    full = jnp.zeros(dims, target.dtype)
+    for mask in range(ways):
+        part = lax.dynamic_slice_in_dim(target, (here ^ mask) * width_2, width_2, axis=2)
+        if mask:
+            part = lax.ppermute(part, "region", [(d, d ^ mask) for d in range(ways)])
+        full = lax.dynamic_update_slice_in_dim(full, part, (here ^ mask) * height, axis=2)
+    received = full
     flipped = (
         received.reshape(stacked, block_rows, devices, block_rows)
         .transpose(0, 3, 2, 1)

time: 1380 us -> 1460 us (1.058)
  starting transfers between devices: 55.9 us -> 249 us
  waiting for transfers between devices: 701 us -> 559 us
  other arithmetic: 127 us -> 144 us
    all_to_all x1 -> x0, waiting for transfers between devices: 568 us -> none  [shards(): lax.all_to_all(target, 'region', split_axis=2, concat_axis=2, tiled=True)]
    ppermute x0 -> x15, waiting for transfers between devices: none -> 501 us  [shards(): part = lax.ppermute(part, 'region', [(d, d ^ mask) for d in range(ways)])]
    ppermute x17, starting transfers between devices: 48.3 us -> 224 us  [shifted(): return lax.ppermute(value, axis, pairs)]
    ppermute x17, waiting for transfers between devices: 133 us -> 57.7 us  [shifted(): return lax.ppermute(value, axis, pairs)]
    dynamic_update_slice x0 -> x16, local copies, waits for them, and re-layouts: none -> 40.5 us  [shards(): lax.dynamic_update_slice_in_dim(full, part, (here ^ mask) * height, axis=2)]
    reshape x1 -> x0, local copies, waits for them, and re-layouts: 31.1 us -> none  [shards(): received.reshape(stacked, block_rows, devices, block_rows)]
    reshape x1, local copies, waits for them, and re-layouts: 50 us -> 22.7 us  [shards(): flipped = received.reshape(stacked, block_rows, devices, block_rows).tran...]
    ppermute x0 -> x15, starting transfers between devices: none -> 24.7 us  [shards(): part = lax.ppermute(part, 'region', [(d, d ^ mask) for d in range(ways)])]
  transfers between devices with their start and end apart: 18 -> 32, of which waited for: 9 -> 13; matrix products, arithmetic and copies ran while one was open for 30% -> 36% of each run, Pallas kernels for 0% -> 0%
where the time goes in v1:
time: 1460 us; the launch traced here: 1450 us
  waiting for transfers between devices  559 us (38%)
  local copies, waits for them, and re-layouts  352 us (24%)
  starting transfers between devices  249 us (17%)
  other arithmetic  144 us (10%)
  matrix products  134 us (9%)
    ppermute x15, waiting for transfers between devices, shards(): part = lax.ppermute(part, 'region', [(d, d ^ mask) for d in range(ways)])  501 us
    ppermute x17, starting transfers between devices, shifted(): return lax.ppermute(value, axis, pairs)  224 us
    add x27, local copies, waits for them, and re-layouts, place_views(): placed + lax.dynamic_update_slice(blank, later_parts[lag_number], (0, lag...  161 us
    unnamed x37, local copies, waits for them, and re-layouts  65.5 us
    ppermute x17, waiting for transfers between devices, shifted(): return lax.ppermute(value, axis, pairs)  57.7 us
    dynamic_update_slice x27, other arithmetic, place_views(): lax.dynamic_update_slice(blank, later_parts[lag_number], (0, lag_steps[la...  55.1 us
    dynamic_update_slice x16, local copies, waits for them, and re-layouts, shards(): lax.dynamic_update_slice_in_dim(full, part, (here ^ mask) * height, axis=2)  40.5 us
    convert_element_type x3, other arithmetic, pair_tiles(): lax.dynamic_slice_in_dim(flipped, column_at, width, 2).astype(jnp.float32)  33.3 us
  transfers between devices with their start and end apart: 32, of which 13 were waited for; matrix products, arithmetic and copies ran while one was open for 36% of the time, Pallas kernels for 0%

profile of v1, /device:TPU:0, one launch (start us, length us, event | category | flops | bytes accessed | tf_op | source)
XLA Modules:
  0.0 1449.0 jit_solution(10780023558870916601)
XLA Ops:
  0.0 24.2 %constant_dynamic-slice_fusion.1 = (bf16[4,512,512]{2,1,0:T(8,128)(2,1)}, bf16[4,512,512]{2,1,0:T(8,128)(2,1)}, bf16[4,512,512]{2,1,0:T(8,128)(2,1)}, bf16[4,512...) fusion(bf16[4,512,8192]{2,1,0:T(8,128)(2,1)} %param.7, ...), kind=kLoop, calls=%fused_computation.204 | loop fusion | flops 1048576 | bytes 71303232 | tf_op jit(solution)/shard_map/dynamic_slice | solution.py:104
  60.9 21.5 %collective-permute-done.9 = bf16[4,512,512]{1,2,0:T(8,128)(2,1)} collective-permute-done((bf16[4,512,512]{1,2,0:T(8,128)(2,1)}, bf16[4,512,512]{1,2,0:T(8,128)(2,1)}, u32[]{:S(2)}, u32[]{:S(2)}) %collective-permute-start.9) | collective-permute-done | bytes 2097184 | tf_op jit(solution)/shard_map/ppermute | solution.py:106
  88.4 38.5 %collective-permute-done.10 = bf16[4,512,512]{1,2,0:T(8,128)(2,1)} collective-permute-done((bf16[4,512,512]{1,2,0:T(8,128)(2,1)}, bf16[4,512,512]{1,2,0:T(8,128)(2,1)}, u32[]{:S(2)}, u32[]{:S(2)}) %collective-permute-start.10) | collective-permute-done | bytes 2097184 | tf_op jit(solution)/shard_map/ppermute | solution.py:106
  138.0 88.5 %collective-permute-done.12 = bf16[4,512,512]{1,2,0:T(8,128)(2,1)} collective-permute-done((bf16[4,512,512]{1,2,0:T(8,128)(2,1)}, bf16[4,512,512]{1,2,0:T(8,128)(2,1)}, u32[]{:S(2)}, u32[]{:S(2)}) %collective-permute-start.12) | collective-permute-done | bytes 2097184 | tf_op jit(solution)/shard_map/ppermute | solution.py:106
  248.9 25.0 %collective-permute-done.13 = bf16[4,512,512]{1,2,0:T(8,128)(2,1)} collective-permute-done((bf16[4,512,512]{1,2,0:T(8,128)(2,1)}, bf16[4,512,512]{1,2,0:T(8,128)(2,1)}, u32[]{:S(2)}, u32[]{:S(2)}) %collective-permute-start.13) | collective-permute-done | bytes 2097184 | tf_op jit(solution)/shard_map/ppermute | solution.py:106
  299.7 17.8 %collective-permute-done.14 = bf16[4,512,512]{1,2,0:T(8,128)(2,1)} collective-permute-done((bf16[4,512,512]{1,2,0:T(8,128)(2,1)}, bf16[4,512,512]{1,2,0:T(8,128)(2,1)}, u32[]{:S(2)}, u32[]{:S(2)}) %collective-permute-start.14) | collective-permute-done | bytes 2097184 | tf_op jit(solution)/shard_map/ppermute | solution.py:106
  321.1 11.0 broadcast_in_dim.7
  341.7 248.0 %collective-permute-done.17 = bf16[4,512,512]{1,2,0:T(8,128)(2,1)} collective-permute-done((bf16[4,512,512]{1,2,0:T(8,128)(2,1)}, bf16[4,512,512]{1,2,0:T(8,128)(2,1)}, u32[]{:S(2)}, u32[]{:S(2)}) %collective-permute-start.17) | collective-permute-done | bytes 2097184 | tf_op jit(solution)/shard_map/ppermute | solution.py:106
  617.9 61.7 %collective-permute-done.18 = bf16[4,512,512]{1,2,0:T(8,128)(2,1)} collective-permute-done((bf16[4,512,512]{1,2,0:T(8,128)(2,1)}, bf16[4,512,512]{1,2,0:T(8,128)(2,1)}, u32[]{:S(2)}, u32[]{:S(2)}) %collective-permute-start.18) | collective-permute-done | bytes 2097184 | tf_op jit(solution)/shard_map/ppermute | solution.py:106
  688.3 22.7 %copy.86 = bf16[4,16,64,8,512]{4,3,1,2,0:T(8,128)(2,1)} copy(bf16[4,16,64,8,512]{4,3,2,1,0:T(8,128)(2,1)} %bitcast.440) | data formatting | bytes 67108864 | tf_op jit(solution)/shard_map/reshape | solution.py:112
  720.9 677.1 %while.23 = (s32[]{:T(128)}, bf16[512,512]{1,0:T(8,128)(2,1)S(1)}, f32[512,512]{1,0:T(8,128)}, f32[512,384]{1,0:T(8,128)}, f32[3,512,384]{2,1,0:T(8,128)}, /*ind...) while((s32[]{:T(128)}, bf16[512,512]{1,0:T(8,128)(2,1)S(1)}, ...), condition=%wide.region_1.2_spmd.clone, body=%wide.region_0.1_spmd.clone.sunk | while | flops 16968056832 | bytes 553650496 | solution.py:141
  722.7 15.5 %dynamic-slice_convert_fusion.10 = (f32[4,512,512]{2,1,0:T(8,128)}, f32[4,512,512]{2,1,0:T(8,128)}, f32[4,512,512]{2,1,0:T(8,128)}, f32[4,512,512]{2,1,0:T(8,128...) fusion(bf16[4,512,8192]{2,1,0:T(8,128)(2,1)} %get-tuple-element, ...), kind=kLoop, calls=%fused_computation.25.clone.1 | loop fusion | flops 8388608 | bytes 50331664 | tf_op jit(solution)/shard_map/while/body/eval_jaxpr/convert_element_type | solution.py:49
  763.1 5.2 add.982
  771.0 5.2 add.983
  778.8 5.2 add.984
  789.5 6.1 collective-permute-done.1
  804.7 6.5 add.986
  813.5 6.5 add.987
  822.3 6.5 add.988
  834.4 202.3 %collective-permute-start.5 = (f32[512,512]{1,0:T(8,128)}, f32[512,512]{1,0:T(8,128)}, u32[]{:S(2)}, u32[]{:S(2)}) collective-permute-start(f32[512,512]{1,0:T(8,128)} %add.985), channel_id=1, source_target_pairs={{0,1},{1,2},{2,3},{3,4},{4,5},{5,6},{6,7},{7,8},{8,9},{9,10},{10,1... | collective-permute-start | bytes 3145736 | tf_op jit(solution)/shard_map/while/body/eval_jaxpr/ppermute | solution.py:15
  1060.1 5.2 add.990
  1067.9 5.2 add.991
  1075.8 5.2 add.992
  1081.0 8.4 collective-permute-start.3
  1111.6 6.5 add.994
  1120.3 6.5 add.995
  1137.6 6.5 add.996
  1147.1 6.1 add_add_fusion.2
  1161.0 15.5 %dynamic-slice_convert_fusion.10 = (f32[4,512,512]{2,1,0:T(8,128)}, f32[4,512,512]{2,1,0:T(8,128)}, f32[4,512,512]{2,1,0:T(8,128)}, f32[4,512,512]{2,1,0:T(8,128...) fusion(bf16[4,512,8192]{2,1,0:T(8,128)(2,1)} %get-tuple-element, ...), kind=kLoop, calls=%fused_computation.25.clone.1 | loop fusion | flops 8388608 | bytes 50331664 | tf_op jit(solution)/shard_map/while/body/eval_jaxpr/convert_element_type | solution.py:49
  1201.4 5.2 add.982
  1209.3 5.2 add.983
  1217.1 5.2 add.984
  1228.0 6.1 collective-permute-done.1
  1243.1 6.5 add.986
  1251.9 6.5 add.987
  1260.7 6.5 add.988
  1276.8 18.8 %collective-permute-done.2 = bf16[512,512]{1,0:T(8,128)(2,1)S(1)} collective-permute-done((bf16[512,512]{1,0:T(8,128)(2,1)S(1)}, bf16[512,512]{1,0:T(8,128)(2,1)S(1)}, u32[]{:S(2)}, u32[]{:S(2)}) %collective-permute-start.2) | collective-permute-done | bytes 524320 | tf_op jit(solution)/shard_map/while/body/eval_jaxpr/ppermute | solution.py:15
  1307.3 5.2 add.990
  1333.3 6.1 collective-permute-done.3
  1353.1 6.5 add.994
  1361.9 6.5 add.995
  1376.7 6.5 add.996
  1386.2 6.1 add_add_fusion.2
  1400.9 6.9 add.786
  1409.2 6.9 add.788
  1417.5 6.9 add.790
  1424.4 15.5 %collective-permute-done.23 = f32[512,512]{1,0:T(8,128)} collective-permute-done((f32[512,512]{1,0:T(8,128)}, f32[512,512]{1,0:T(8,128)}, u32[]{:S(2)}, u32[]{:S(2)}) %collective-permute-start.23) | collective-permute-done | bytes 1048608 | tf_op jit(solution)/shard_map/ppermute | solution.py:15
  1442.4 6.1 dynamic_update_slice.139
  (371 shorter events, 415.1 us)
Async XLA Ops:
  28.4 25.8 %collective-permute-start.8 = (bf16[4,512,512]{1,2,0:T(8,128)(2,1)}, bf16[4,512,512]{1,2,0:T(8,128)(2,1)}, u32[]{:S(2)}, u32[]{:S(2)}) collective-permute-start(bf16[4,512,512]{1,2,0:T(8,128)(2,1)} %copy.71), channel_id=1, source_target_pairs={{0,1},{1,0},{2,3},{3,2},{4,5},{5,4},{6,7},{7,6},{8,9},{9,8},{10,11... | collective-permute-start | bytes 6291464 | tf_op jit(solution)/shard_map/ppermute | solution.py:106
  33.0 49.3 %collective-permute-start.9 = (bf16[4,512,512]{1,2,0:T(8,128)(2,1)}, bf16[4,512,512]{1,2,0:T(8,128)(2,1)}, u32[]{:S(2)}, u32[]{:S(2)}) collective-permute-start(bf16[4,512,512]{1,2,0:T(8,128)(2,1)} %copy.72), channel_id=1, source_target_pairs={{0,2},{1,3},{2,0},{3,1},{4,6},{5,7},{6,4},{7,5},{8,10},{9,11},{10,... | collective-permute-start | bytes 6291464 | tf_op jit(solution)/shard_map/ppermute | solution.py:106
  39.7 87.2 %collective-permute-start.10 = (bf16[4,512,512]{1,2,0:T(8,128)(2,1)}, bf16[4,512,512]{1,2,0:T(8,128)(2,1)}, u32[]{:S(2)}, u32[]{:S(2)}) collective-permute-start(bf16[4,512,512]{1,2,0:T(8,128)(2,1)} %copy.73), channel_id=1, source_target_pairs={{0,3},{1,2},{2,1},{3,0},{4,7},{5,6},{6,5},{7,4},{8,11},{9,10},{10,... | collective-permute-start | bytes 6291464 | tf_op jit(solution)/shard_map/ppermute | solution.py:106
  44.0 89.7 %collective-permute-start.11 = (bf16[4,512,512]{1,2,0:T(8,128)(2,1)}, bf16[4,512,512]{1,2,0:T(8,128)(2,1)}, u32[]{:S(2)}, u32[]{:S(2)}) collective-permute-start(bf16[4,512,512]{1,2,0:T(8,128)(2,1)} %copy.74), channel_id=1, source_target_pairs={{0,4},{1,5},{2,6},{3,7},{4,0},{5,1},{6,2},{7,3},{8,12},{9,13},{10,... | collective-permute-start | bytes 6291464 | tf_op jit(solution)/shard_map/ppermute | solution.py:106
  50.0 176.5 %collective-permute-start.12 = (bf16[4,512,512]{1,2,0:T(8,128)(2,1)}, bf16[4,512,512]{1,2,0:T(8,128)(2,1)}, u32[]{:S(2)}, u32[]{:S(2)}) collective-permute-start(bf16[4,512,512]{1,2,0:T(8,128)(2,1)} %copy.75), channel_id=1, source_target_pairs={{0,5},{1,4},{2,7},{3,6},{4,1},{5,0},{6,3},{7,2},{8,13},{9,12},{10,... | collective-permute-start | bytes 6291464 | tf_op jit(solution)/shard_map/ppermute | solution.py:106
  54.1 219.7 %collective-permute-start.13 = (bf16[4,512,512]{1,2,0:T(8,128)(2,1)}, bf16[4,512,512]{1,2,0:T(8,128)(2,1)}, u32[]{:S(2)}, u32[]{:S(2)}) collective-permute-start(bf16[4,512,512]{1,2,0:T(8,128)(2,1)} %copy.76), channel_id=1, source_target_pairs={{0,6},{1,7},{2,4},{3,5},{4,2},{5,3},{6,0},{7,1},{8,14},{9,15},{10,... | collective-permute-start | bytes 6291464 | tf_op jit(solution)/shard_map/ppermute | solution.py:106
  82.3 235.2 %collective-permute-start.14 = (bf16[4,512,512]{1,2,0:T(8,128)(2,1)}, bf16[4,512,512]{1,2,0:T(8,128)(2,1)}, u32[]{:S(2)}, u32[]{:S(2)}) collective-permute-start(bf16[4,512,512]{1,2,0:T(8,128)(2,1)} %copy.77), channel_id=1, source_target_pairs={{0,7},{1,6},{2,5},{3,4},{4,3},{5,2},{6,1},{7,0},{8,15},{9,14},{10,... | collective-permute-start | bytes 6291464 | tf_op jit(solution)/shard_map/ppermute | solution.py:106
  126.9 206.6 %collective-permute-start.15 = (bf16[4,512,512]{1,2,0:T(8,128)(2,1)}, bf16[4,512,512]{1,2,0:T(8,128)(2,1)}, u32[]{:S(2)}, u32[]{:S(2)}) collective-permute-start(bf16[4,512,512]{1,2,0:T(8,128)(2,1)} %copy.78), channel_id=1, source_target_pairs={{0,8},{1,9},{2,10},{3,11},{4,12},{5,13},{6,14},{7,15},{8,0},{9,1},... | collective-permute-start | bytes 6291464 | tf_op jit(solution)/shard_map/ppermute | solution.py:106
  133.7 201.4 %collective-permute-start.16 = (bf16[4,512,512]{1,2,0:T(8,128)(2,1)}, bf16[4,512,512]{1,2,0:T(8,128)(2,1)}, u32[]{:S(2)}, u32[]{:S(2)}) collective-permute-start(bf16[4,512,512]{1,2,0:T(8,128)(2,1)} %copy.79), channel_id=1, source_target_pairs={{0,9},{1,8},{2,11},{3,10},{4,13},{5,12},{6,15},{7,14},{8,1},{9,0},... | collective-permute-start | bytes 6291464 | tf_op jit(solution)/shard_map/ppermute | solution.py:106
  133.8 96.7 %copy-start.41 = (s32[3]{0:T(128)S(1)}, s32[3]{0:T(128)}, u32[]{:S(2)}) copy-start(s32[3]{0:T(128)} %param.9) | copy-start | bytes 40
  226.5 363.3 %collective-permute-start.17 = (bf16[4,512,512]{1,2,0:T(8,128)(2,1)}, bf16[4,512,512]{1,2,0:T(8,128)(2,1)}, u32[]{:S(2)}, u32[]{:S(2)}) collective-permute-start(bf16[4,512,512]{1,2,0:T(8,128)(2,1)} %copy.80), channel_id=1, source_target_pairs={{0,10},{1,11},{2,8},{3,9},{4,14},{5,15},{6,12},{7,13},{8,2},{9,3},... | collective-permute-start | bytes 6291464 | tf_op jit(solution)/shard_map/ppermute | solution.py:106
  235.1 6.9 copy-start.35
  273.9 405.7 %collective-permute-start.18 = (bf16[4,512,512]{1,2,0:T(8,128)(2,1)}, bf16[4,512,512]{1,2,0:T(8,128)(2,1)}, u32[]{:S(2)}, u32[]{:S(2)}) collective-permute-start(bf16[4,512,512]{1,2,0:T(8,128)(2,1)} %copy.81), channel_id=1, source_target_pairs={{0,11},{1,10},{2,9},{3,8},{4,15},{5,14},{6,13},{7,12},{8,3},{9,2},... | collective-permute-start | bytes 6291464 | tf_op jit(solution)/shard_map/ppermute | solution.py:106
  299.5 18.0 %copy-start.40 = (bf16[4,512,512]{1,2,0:T(8,128)(2,1)S(1)}, bf16[4,512,512]{1,2,0:T(8,128)(2,1)}, u32[]{:S(2)}) copy-start(bf16[4,512,512]{1,2,0:T(8,128)(2,1)} %copy.82) | copy-start | bytes 6291460
  299.7 32.4 %copy-start.34 = (bf16[4,512,512]{1,2,0:T(8,128)(2,1)S(1)}, bf16[4,512,512]{1,2,0:T(8,128)(2,1)}, u32[]{:S(2)}) copy-start(bf16[4,512,512]{1,2,0:T(8,128)(2,1)} %copy.40) | copy-start | bytes 6291460
  317.5 365.1 %collective-permute-start.19 = (bf16[4,512,512]{1,2,0:T(8,128)(2,1)S(1)}, bf16[4,512,512]{1,2,0:T(8,128)(2,1)S(1)}, u32[]{:S(2)}, u32[]{:S(2)}) collective-permute-start(bf16[4,512,512]{1,2,0:T(8,128)(2,1)S(1)} %copy-done.40), channel_id=1, source_target_pairs={{0,12},{1,13},{2,14},{3,15},{4,8},{5,9},{6,10},{7,11},{8,4},{9,5},... | collective-permute-start | bytes 6291464 | tf_op jit(solution)/shard_map/ppermute | solution.py:106
  334.4 349.6 %collective-permute-start.20 = (bf16[4,512,512]{1,2,0:T(8,128)(2,1)S(1)}, bf16[4,512,512]{1,2,0:T(8,128)(2,1)S(1)}, u32[]{:S(2)}, u32[]{:S(2)}) collective-permute-start(bf16[4,512,512]{1,2,0:T(8,128)(2,1)S(1)} %copy-done.39), channel_id=1, source_target_pairs={{0,13},{1,12},{2,15},{3,14},{4,9},{5,8},{6,11},{7,10},{8,5},{9,4},... | collective-permute-start | bytes 6291464 | tf_op jit(solution)/shard_map/ppermute | solution.py:106
  335.1 254.7 %copy-start.37 = (bf16[4,512,512]{1,2,0:T(8,128)(2,1)S(1)}, bf16[4,512,512]{1,2,0:T(8,128)(2,1)}, u32[]{:S(2)}) copy-start(bf16[4,512,512]{1,2,0:T(8,128)(2,1)} %copy.85) | copy-start | bytes 6291460
  335.1 350.4 %collective-permute-start.21 = (bf16[4,512,512]{1,2,0:T(8,128)(2,1)S(1)}, bf16[4,512,512]{1,2,0:T(8,128)(2,1)S(1)}, u32[]{:S(2)}, u32[]{:S(2)}) collective-permute-start(bf16[4,512,512]{1,2,0:T(8,128)(2,1)S(1)} %copy-done.38), channel_id=1, source_target_pairs={{0,14},{1,15},{2,12},{3,13},{4,10},{5,11},{6,8},{7,9},{8,6},{9,7},... | collective-permute-start | bytes 6291464 | tf_op jit(solution)/shard_map/ppermute | solution.py:106
  589.7 97.2 %collective-permute-start.22 = (bf16[4,512,512]{1,2,0:T(8,128)(2,1)S(1)}, bf16[4,512,512]{1,2,0:T(8,128)(2,1)S(1)}, u32[]{:S(2)}, u32[]{:S(2)}) collective-permute-start(bf16[4,512,512]{1,2,0:T(8,128)(2,1)S(1)} %copy-done.37), channel_id=1, source_target_pairs={{0,15},{1,14},{2,13},{3,12},{4,11},{5,10},{6,9},{7,8},{8,7},{9,6},... | collective-permute-start | bytes 6291464 | tf_op jit(solution)/shard_map/ppermute | solution.py:106
  720.9 17.3 %collective-permute-start = (bf16[512,512]{1,0:T(8,128)(2,1)S(1)}, bf16[512,512]{1,0:T(8,128)(2,1)S(1)}, u32[]{:S(2)}, u32[]{:S(2)}) collective-permute-start(bf16[512,512]{1,0:T(8,128)(2,1)S(1)} %get-tuple-element.623), channel_id=1, source_target_pairs={{0,1},{1,2},{2,3},{3,4},{4,5},{5,6},{6,7},{7,8},{8,9},{9,10},{10,1... | collective-permute-start | bytes 1572872 | tf_op jit(solution)/shard_map/while/body/eval_jaxpr/ppermute | solution.py:15
  722.1 109.7 %collective-permute-start.4 = (f32[512,512]{1,0:T(8,128)}, f32[512,512]{1,0:T(8,128)}, u32[]{:S(2)}, u32[]{:S(2)}) collective-permute-start(f32[512,512]{1,0:T(8,128)} %broadcast_select_fusion.2), channel_id=1, source_target_pairs={{0,1},{1,2},{2,3},{3,4},{4,5},{5,6},{6,7},{7,8},{8,9},{9,10},{10,1... | collective-permute-start | bytes 3145736 | tf_op jit(solution)/shard_map/while/body/eval_jaxpr/ppermute | solution.py:15
  784.0 11.6 collective-permute-start.1
  787.1 8.5 copy-start.2
  831.8 207.7 %copy-start.23 = (bf16[512,512]{1,0:T(8,128)(2,1)S(1)}, bf16[512,512]{1,0:T(8,128)(2,1)}, u32[]{:S(2)}) copy-start(bf16[512,512]{1,0:T(8,128)(2,1)} %copy-done.22) | copy-start | bytes 1572868 | tf_op jit(solution)/shard_map/while
  831.8 207.7 %copy-start.24 = (f32[512,384]{1,0:T(8,128)S(1)}, f32[512,384]{1,0:T(8,128)}, u32[]{:S(2)}) copy-start(f32[512,384]{1,0:T(8,128)} %fusion.356) | copy-start | bytes 2359300 | tf_op jit(solution)/shard_map/while
  834.4 206.5 %copy-start.15 = (bf16[3,512,512]{2,1,0:T(8,128)(2,1)S(1)}, bf16[3,512,512]{2,1,0:T(8,128)(2,1)}, u32[]{:S(2)}) copy-start(bf16[3,512,512]{2,1,0:T(8,128)(2,1)} %copy-done.14) | copy-start | bytes 4718596 | tf_op jit(solution)/shard_map/while
  834.4 265.7 %collective-permute-start.5 = (f32[512,512]{1,0:T(8,128)}, f32[512,512]{1,0:T(8,128)}, u32[]{:S(2)}, u32[]{:S(2)}) collective-permute-start(f32[512,512]{1,0:T(8,128)} %add.985), channel_id=1, source_target_pairs={{0,1},{1,2},{2,3},{3,4},{4,5},{5,6},{6,7},{7,8},{8,9},{9,10},{10,1... | collective-permute-start | bytes 3145736 | tf_op jit(solution)/shard_map/while/body/eval_jaxpr/ppermute | solution.py:15
  1036.7 11.7 collective-permute-start.2
  1040.9 8.0 copy-start.12
  1052.9 6.0 copy-start.8
  1081.0 11.0 copy-start.17
  1081.0 13.4 collective-permute-start.3
  1103.0 27.4 %collective-permute-start.6 = (f32[512,512]{1,0:T(8,128)}, f32[512,512]{1,0:T(8,128)}, u32[]{:S(2)}, u32[]{:S(2)}) collective-permute-start(f32[512,512]{1,0:T(8,128)} %add.989), channel_id=1, source_target_pairs={{0,1},{1,2},{2,3},{3,4},{4,5},{5,6},{6,7},{7,8},{8,9},{9,10},{10,1... | collective-permute-start | bytes 3145736 | tf_op jit(solution)/shard_map/while/body/eval_jaxpr/ppermute | solution.py:15
  1132.8 20.5 %collective-permute-start.7 = (f32[512,512]{1,0:T(8,128)}, f32[512,512]{1,0:T(8,128)}, u32[]{:S(2)}, u32[]{:S(2)}) collective-permute-start(f32[512,512]{1,0:T(8,128)} %add.993), channel_id=1, source_target_pairs={{0,1},{1,2},{2,3},{3,4},{4,5},{5,6},{6,7},{7,8},{8,9},{9,10},{10,1... | collective-permute-start | bytes 3145736 | tf_op jit(solution)/shard_map/while/body/eval_jaxpr/ppermute | solution.py:15
  1155.9 20.7 %collective-permute-start = (bf16[512,512]{1,0:T(8,128)(2,1)S(1)}, bf16[512,512]{1,0:T(8,128)(2,1)S(1)}, u32[]{:S(2)}, u32[]{:S(2)}) collective-permute-start(bf16[512,512]{1,0:T(8,128)(2,1)S(1)} %get-tuple-element.623), channel_id=1, source_target_pairs={{0,1},{1,2},{2,3},{3,4},{4,5},{5,6},{6,7},{7,8},{8,9},{9,10},{10,1... | collective-permute-start | bytes 1572872 | tf_op jit(solution)/shard_map/while/body/eval_jaxpr/ppermute | solution.py:15
  1158.2 112.1 %collective-permute-start.4 = (f32[512,512]{1,0:T(8,128)}, f32[512,512]{1,0:T(8,128)}, u32[]{:S(2)}, u32[]{:S(2)}) collective-permute-start(f32[512,512]{1,0:T(8,128)} %broadcast_select_fusion.2), channel_id=1, source_target_pairs={{0,1},{1,2},{2,3},{3,4},{4,5},{5,6},{6,7},{7,8},{8,9},{9,10},{10,1... | collective-permute-start | bytes 3145736 | tf_op jit(solution)/shard_map/while/body/eval_jaxpr/ppermute | solution.py:15
  1222.4 11.7 collective-permute-start.1
  1225.6 8.5 copy-start.2
  1272.8 71.8 %collective-permute-start.5 = (f32[512,512]{1,0:T(8,128)}, f32[512,512]{1,0:T(8,128)}, u32[]{:S(2)}, u32[]{:S(2)}) collective-permute-start(f32[512,512]{1,0:T(8,128)} %add.985), channel_id=1, source_target_pairs={{0,1},{1,2},{2,3},{3,4},{4,5},{5,6},{6,7},{7,8},{8,9},{9,10},{10,1... | collective-permute-start | bytes 3145736 | tf_op jit(solution)/shard_map/while/body/eval_jaxpr/ppermute | solution.py:15
  1272.8 22.7 %collective-permute-start.2 = (bf16[512,512]{1,0:T(8,128)(2,1)S(1)}, bf16[512,512]{1,0:T(8,128)(2,1)S(1)}, u32[]{:S(2)}, u32[]{:S(2)}) collective-permute-start(bf16[512,512]{1,0:T(8,128)(2,1)S(1)} %collective-permute-done.1), channel_id=1, source_target_pairs={{0,1},{1,2},{2,3},{3,4},{4,5},{5,6},{6,7},{7,8},{8,9},{9,10},{10,1... | collective-permute-start | bytes 1572872 | tf_op jit(solution)/shard_map/while/body/eval_jaxpr/ppermute | solution.py:15
  1274.3 21.8 %copy-start.12 = (f32[4,512,512]{2,1,0:T(8,128)S(1)}, f32[4,512,512]{2,1,0:T(8,128)}, u32[]{:S(2)}) copy-start(f32[4,512,512]{2,1,0:T(8,128)} %get-tuple-element.586) | copy-start | bytes 12582916 | tf_op jit(solution)/shard_map/while
  1300.1 6.0 copy-start.8
  1328.2 11.3 collective-permute-start.3
  1331.0 8.5 copy-start
  1347.6 24.3 %collective-permute-start.6 = (f32[512,512]{1,0:T(8,128)}, f32[512,512]{1,0:T(8,128)}, u32[]{:S(2)}, u32[]{:S(2)}) collective-permute-start(f32[512,512]{1,0:T(8,128)} %add.989), channel_id=1, source_target_pairs={{0,1},{1,2},{2,3},{3,4},{4,5},{5,6},{6,7},{7,8},{8,9},{9,10},{10,1... | collective-permute-start | bytes 3145736 | tf_op jit(solution)/shard_map/while/body/eval_jaxpr/ppermute | solution.py:15
  1374.4 18.0 %collective-permute-start.7 = (f32[512,512]{1,0:T(8,128)}, f32[512,512]{1,0:T(8,128)}, u32[]{:S(2)}, u32[]{:S(2)}) collective-permute-start(f32[512,512]{1,0:T(8,128)} %add.993), channel_id=1, source_target_pairs={{0,1},{1,2},{2,3},{3,4},{4,5},{5,6},{6,7},{7,8},{8,9},{9,10},{10,1... | collective-permute-start | bytes 3145736 | tf_op jit(solution)/shard_map/while/body/eval_jaxpr/ppermute | solution.py:15
  1398.1 41.8 %collective-permute-start.23 = (f32[512,512]{1,0:T(8,128)}, f32[512,512]{1,0:T(8,128)}, u32[]{:S(2)}, u32[]{:S(2)}) collective-permute-start(f32[512,512]{1,0:T(8,128)} %get-tuple-element.357), channel_id=1, source_target_pairs={{0,8},{1,9},{2,10},{3,11},{4,12},{5,13},{6,14},{7,15},{8,0},{9,1},... | collective-permute-start | bytes 3145736 | tf_op jit(solution)/shard_map/ppermute | solution.py:15
  (57 other events, 116.9 us)
